TPU v7x, 128 devices: a whole 4x4x4 slice. The times are simulated.
128 devices in a mesh: ang: 16 (over z_lo, x, core), img: 8 (over z_hi, y).
Axes of the slice: x: 4, y: 4, z: 4 (z_hi: 2, z_lo: 2; z = z_hi * 2 + z_lo), core: 2. Of those that a mesh axis runs over, the one named last changes fastest.
Arguments:
- sinogram: bfloat16 [32, 64, 4096], P('ang', None, 'img'), may hold values from -4 to 28
- offsets: int32 [32], replicated, may hold values from 0 to 65504, as said below
- steps: int32 [32, 2], replicated, may hold values from -32 to 32, as said below
Outputs:
- picture: bfloat16 [1024, 64, 1024], P('ang', None, 'img')
Inputs may be any that keep to these rules, and one draw needn't show every extreme that they name: Each row (u, v) of steps satisfies u^2 + v^2 <= 32^2 < (|u| + 1)^2 + (|v| + 1)^2. For every angle a and every pixel (y, x) with 0 <= x, y < 1024, offsets[a] + steps[a, 0] x + steps[a, 1] y lies in 0 to 65504.
All inputs are finite; a program needn't handle non-finite values.
Results may differ from a plain program's by a relative error of at most 0.0053.
Values may be sent and summed in bfloat16 or wider, within the bound.
A program may use at most 192 MiB of HBM per device.

v0:
```python
import math
import jax
import jax.numpy as jnp
from jax import lax
from jax.sharding import Mesh
from jax.sharding import PartitionSpec as P

BINS = 4096
IMG = 1024
TILE = 32
BAND = 128
IMG_AXES = ("img_0", "img_1")


def in_order(blocks, dim):
    shape = list(blocks.shape[1:])
    shape[dim] *= blocks.shape[0]
    return jnp.moveaxis(blocks, 0, dim).reshape(shape)


def stacked_from(array, axes, sequence):
    blocks = array
    for k in sequence:
        blocks = lax.all_gather(blocks, axes[k])
    done = sequence[::-1]
    back = [done.index(k) for k in range(len(axes))]
    blocks = blocks.transpose(*back, *range(len(axes), blocks.ndim))
    return blocks.reshape(-1, *array.shape)


def gathered_by_axis(array, axes, sequence, dim):
    return in_order(stacked_from(array, axes, sequence), dim)


def ramp_table():
    bin_index = jnp.arange(BINS, dtype=jnp.int32)
    offset_gap = bin_index[None, :] - bin_index[:, None]
    safe_gap = jnp.where(offset_gap == 0, 1, offset_gap).astype(jnp.float32)
    odd_gap = offset_gap % 2 != 0
    kernel = jnp.where(
        offset_gap == 0,
        jnp.float32(0.25),
        jnp.where(odd_gap, -1.0 / (math.pi**2 * safe_gap * safe_gap), jnp.float32(0.0)),
    )
    return kernel


def project_block(filtered, geo_offsets, geo_steps, row_top, row_count, col_left, col_count):
    slices = filtered.shape[1]
    across = col_count // TILE
    block_rows = min(row_count, 8 * TILE)
    while row_count % block_rows:
        block_rows = block_rows - TILE
    tiles_down = block_rows // TILE
    tile_count = tiles_down * across
    tile_order = jnp.arange(tile_count, dtype=jnp.int32)
    tile_top = tile_order // across * TILE
    tile_left = tile_order % across * TILE + col_left
    in_tile = jnp.arange(TILE * TILE, dtype=jnp.int32)
    pix_row = in_tile // TILE
    pix_col = in_tile % TILE
    band_slot = jnp.arange(BAND, dtype=jnp.int32)[None, :, None]

    def one_block(block_no):
        block_top = row_top + block_no * block_rows

        def one_angle(summed, angle_data):
            filtered_one, offset, step_pair = angle_data
            step_x = step_pair[0]
            step_y = step_pair[1]
            corner = offset + step_x * tile_left + step_y * (block_top + tile_top)
            corner = (
                corner + jnp.minimum(step_x, 0) * (TILE - 1) + jnp.minimum(step_y, 0) * (TILE - 1)
            )
            band_start = jnp.minimum(corner // 16, BINS - BAND)
            band_rows = jax.vmap(
                lambda begin_at: lax.dynamic_slice_in_dim(filtered_one, begin_at, BAND, 1)
            )(band_start)
            position = (
                offset
                + step_x * (tile_left[:, None] + pix_col[None, :])
                + step_y * (block_top + tile_top[:, None] + pix_row[None, :])
            )
            low_bin = (position // 16 - band_start[:, None])[:, None, :]
            upper_weight = ((position % 16).astype(jnp.float32) / 16.0)[:, None, :]
            weights = jnp.where(band_slot == low_bin, 1.0 - upper_weight, 0.0) + jnp.where(
                band_slot == low_bin + 1, upper_weight, 0.0
            )
            weights = weights.astype(jnp.bfloat16)
            contrib = jnp.einsum(
                "tsb,tbp->tsp", band_rows, weights, preferred_element_type=jnp.float32
            )
            return (summed + contrib, None)

        start_sum = jnp.zeros((tile_count, slices, TILE * TILE), jnp.float32)
        summed = lax.scan(one_angle, start_sum, (filtered, geo_offsets, geo_steps))[0]
        summed = summed.reshape(tiles_down, across, slices, TILE, TILE)
        return jnp.transpose(summed, (0, 3, 2, 1, 4)).reshape(block_rows, slices, col_count)

    blocks = lax.map(one_block, jnp.arange(row_count // block_rows, dtype=jnp.int32))
    return blocks.reshape(row_count, slices, col_count)


def shards(sinogram, offsets, steps):
    angles_dev = sinogram.shape[0]
    ramp_rows = ramp_table()
    whole_bins = gathered_by_axis(sinogram, IMG_AXES, (0, 1), 2)
    result = jnp.dot(
        whole_bins.reshape(-1, BINS).astype(jnp.float32),
        ramp_rows,
        precision=lax.Precision.HIGHEST,
        preferred_element_type=jnp.float32,
    )
    filtered = result.astype(jnp.bfloat16).reshape(whole_bins.shape[0], whole_bins.shape[1], BINS)
    ang_count = lax.axis_size("ang")
    img_count = lax.axis_size(IMG_AXES)
    rows_dev = IMG // ang_count
    cols_dev = IMG // img_count
    col_left = lax.axis_index(IMG_AXES) * cols_dev
    total_angles = angles_dev * ang_count
    row_first = lax.axis_index("ang") * rows_dev
    partial_value = project_block(
        lax.all_gather(filtered, "ang", axis=0, tiled=True),
        offsets,
        steps,
        row_first,
        rows_dev,
        col_left,
        cols_dev,
    )
    return (partial_value * (2.0 / math.sqrt(total_angles))).astype(jnp.bfloat16)


def solution(mesh):
    finer = Mesh(mesh.devices.reshape(mesh.shape["ang"], 2, 4), ("ang", "img_0", "img_1"))
    return jax.shard_map(
        shards,
        mesh=finer,
        in_specs=(P("ang", None, IMG_AXES), P(), P()),
        out_specs=P("ang", None, IMG_AXES),
        check_vma=False,
    )
```

profile of v0, /device:TPU:1, one launch (start us, length us, event | category | flops | bytes accessed | tf_op | source)
XLA Modules:
  0.0 874.8 jit_solution(12078001420684586321)
XLA Ops:
  6.5 10.1 %all-gather = bf16[4,64,512]{2,1,0:T(8,128)(2,1)} all-gather(bf16[2,64,512]{2,1,0:T(8,128)(2,1)} %param.5), channel_id=2, replica_groups=mesh['ang'=16,'img_0'=2,'img_1'=4] {'img_0'}, dimensions={0}, use_global_device_ids=true | all-gather | bytes 393216 | tf_op jit(solution)/shard_map/all_gather | solution.py:24
  16.7 24.0 %all-gather.7.cloned.1.call-done = bf16[8,2,64,512]{3,2,1,0:T(8,128)(2,1)} async-done(((bf16[2,2,64,512]{3,2,1,0:T(8,128)(2,1)}), bf16[8,2,64,512]{3,2,1,0:T(8,128)(2,1)}) %all-gather.7.cloned.1.call-update) | async-done | bytes 1048592 | tf_op jit(solution)/shard_map/all_gather | solution.py:24
  43.1 76.2 %fusion.51 = bf16[4096,128]{0,1:T(8,128)(2,1)} fusion(bf16[128,4096]{1,0:T(8,128)(2,1)S(1)} %bitcast.59), kind=kOutput, calls=%fused_computation.89 | convolution fusion | flops 26122649600 | bytes 2097152 | tf_op jit(solution)/shard_map/dot_general | solution.py:108
  119.3 93.4 %all-gather.5.cloned.1.call-done = bf16[32,64,4096]{2,1,0:T(8,128)(2,1)} async-done(((bf16[2,64,4096]{2,1,0:T(8,128)(2,1)}), bf16[32,64,4096]{2,1,0:T(8,128)(2,1)}) %all-gather.5.cloned.1.call-update) | async-done | bytes 16777232 | tf_op jit(solution)/shard_map/all_gather | solution.py:123
  212.7 647.6 %while.27 = (s32[]{:T(128)}, f32[8,64,1024]{2,1,0:T(8,128)S(1)}, bf16[32,64,4096]{2,1,0:T(8,128)(2,1)}, s32[32]{0:T(128)S(1)}, s32[32,2]{0,1:T(2,128)S(1)}, /*in...) while((s32[]{:T(128)}, f32[8,64,1024]{2,1,0:T(8,128)S(1)}, ...), condition=%wide.region_1.2_spmd.clone.clone, body=%wide.region_0.1_spmd.clone.clone.sunk | while | flops 141922896 | bytes 5694332 | solution.py:96
  221.8 9.7 %while.28 = (s32[]{:T(128)}, bf16[64,4096]{1,0:T(8,128)(2,1)S(1)}, s32[8,2]{0,1:T(2,128)S(1)}, bf16[8,64,128]{2,1,0:T(8,128)(2,1)S(1)}, s32[]{:T(128)}) while((s32[]{:T(128)}, bf16[64,4096]{1,0:T(8,128)(2,1)S(1)}, s32[8,2]{0,1:T(2,128)S(1)}, bf16[8,64,128]{2,1,0:T(8,128)(2,1)S(1)}, s32[]{:T(128)}) %tuple.73), condition=%wide.while_cond, body=%wide.while_body.sunk | while | flops 2 | bytes 32873 | solution.py:77
  242.1 9.7 %while.28 = (s32[]{:T(128)}, bf16[64,4096]{1,0:T(8,128)(2,1)S(1)}, s32[8,2]{0,1:T(2,128)S(1)}, bf16[8,64,128]{2,1,0:T(8,128)(2,1)S(1)}, s32[]{:T(128)}) while((s32[]{:T(128)}, bf16[64,4096]{1,0:T(8,128)(2,1)S(1)}, s32[8,2]{0,1:T(2,128)S(1)}, bf16[8,64,128]{2,1,0:T(8,128)(2,1)S(1)}, s32[]{:T(128)}) %tuple.73), condition=%wide.while_cond, body=%wide.while_body.sunk | while | flops 2 | bytes 32873 | solution.py:77
  262.3 9.7 %while.28 = (s32[]{:T(128)}, bf16[64,4096]{1,0:T(8,128)(2,1)S(1)}, s32[8,2]{0,1:T(2,128)S(1)}, bf16[8,64,128]{2,1,0:T(8,128)(2,1)S(1)}, s32[]{:T(128)}) while((s32[]{:T(128)}, bf16[64,4096]{1,0:T(8,128)(2,1)S(1)}, s32[8,2]{0,1:T(2,128)S(1)}, bf16[8,64,128]{2,1,0:T(8,128)(2,1)S(1)}, s32[]{:T(128)}) %tuple.73), condition=%wide.while_cond, body=%wide.while_body.sunk | while | flops 2 | bytes 32873 | solution.py:77
  282.5 9.7 %while.28 = (s32[]{:T(128)}, bf16[64,4096]{1,0:T(8,128)(2,1)S(1)}, s32[8,2]{0,1:T(2,128)S(1)}, bf16[8,64,128]{2,1,0:T(8,128)(2,1)S(1)}, s32[]{:T(128)}) while((s32[]{:T(128)}, bf16[64,4096]{1,0:T(8,128)(2,1)S(1)}, s32[8,2]{0,1:T(2,128)S(1)}, bf16[8,64,128]{2,1,0:T(8,128)(2,1)S(1)}, s32[]{:T(128)}) %tuple.73), condition=%wide.while_cond, body=%wide.while_body.sunk | while | flops 2 | bytes 32873 | solution.py:77
  302.8 9.7 %while.28 = (s32[]{:T(128)}, bf16[64,4096]{1,0:T(8,128)(2,1)S(1)}, s32[8,2]{0,1:T(2,128)S(1)}, bf16[8,64,128]{2,1,0:T(8,128)(2,1)S(1)}, s32[]{:T(128)}) while((s32[]{:T(128)}, bf16[64,4096]{1,0:T(8,128)(2,1)S(1)}, s32[8,2]{0,1:T(2,128)S(1)}, bf16[8,64,128]{2,1,0:T(8,128)(2,1)S(1)}, s32[]{:T(128)}) %tuple.73), condition=%wide.while_cond, body=%wide.while_body.sunk | while | flops 2 | bytes 32873 | solution.py:77
  323.0 9.7 %while.28 = (s32[]{:T(128)}, bf16[64,4096]{1,0:T(8,128)(2,1)S(1)}, s32[8,2]{0,1:T(2,128)S(1)}, bf16[8,64,128]{2,1,0:T(8,128)(2,1)S(1)}, s32[]{:T(128)}) while((s32[]{:T(128)}, bf16[64,4096]{1,0:T(8,128)(2,1)S(1)}, s32[8,2]{0,1:T(2,128)S(1)}, bf16[8,64,128]{2,1,0:T(8,128)(2,1)S(1)}, s32[]{:T(128)}) %tuple.73), condition=%wide.while_cond, body=%wide.while_body.sunk | while | flops 2 | bytes 32873 | solution.py:77
  343.2 9.7 %while.28 = (s32[]{:T(128)}, bf16[64,4096]{1,0:T(8,128)(2,1)S(1)}, s32[8,2]{0,1:T(2,128)S(1)}, bf16[8,64,128]{2,1,0:T(8,128)(2,1)S(1)}, s32[]{:T(128)}) while((s32[]{:T(128)}, bf16[64,4096]{1,0:T(8,128)(2,1)S(1)}, s32[8,2]{0,1:T(2,128)S(1)}, bf16[8,64,128]{2,1,0:T(8,128)(2,1)S(1)}, s32[]{:T(128)}) %tuple.73), condition=%wide.while_cond, body=%wide.while_body.sunk | while | flops 2 | bytes 32873 | solution.py:77
  363.5 9.7 %while.28 = (s32[]{:T(128)}, bf16[64,4096]{1,0:T(8,128)(2,1)S(1)}, s32[8,2]{0,1:T(2,128)S(1)}, bf16[8,64,128]{2,1,0:T(8,128)(2,1)S(1)}, s32[]{:T(128)}) while((s32[]{:T(128)}, bf16[64,4096]{1,0:T(8,128)(2,1)S(1)}, s32[8,2]{0,1:T(2,128)S(1)}, bf16[8,64,128]{2,1,0:T(8,128)(2,1)S(1)}, s32[]{:T(128)}) %tuple.73), condition=%wide.while_cond, body=%wide.while_body.sunk | while | flops 2 | bytes 32873 | solution.py:77
  383.7 9.7 %while.28 = (s32[]{:T(128)}, bf16[64,4096]{1,0:T(8,128)(2,1)S(1)}, s32[8,2]{0,1:T(2,128)S(1)}, bf16[8,64,128]{2,1,0:T(8,128)(2,1)S(1)}, s32[]{:T(128)}) while((s32[]{:T(128)}, bf16[64,4096]{1,0:T(8,128)(2,1)S(1)}, s32[8,2]{0,1:T(2,128)S(1)}, bf16[8,64,128]{2,1,0:T(8,128)(2,1)S(1)}, s32[]{:T(128)}) %tuple.73), condition=%wide.while_cond, body=%wide.while_body.sunk | while | flops 2 | bytes 32873 | solution.py:77
  404.0 9.7 %while.28 = (s32[]{:T(128)}, bf16[64,4096]{1,0:T(8,128)(2,1)S(1)}, s32[8,2]{0,1:T(2,128)S(1)}, bf16[8,64,128]{2,1,0:T(8,128)(2,1)S(1)}, s32[]{:T(128)}) while((s32[]{:T(128)}, bf16[64,4096]{1,0:T(8,128)(2,1)S(1)}, s32[8,2]{0,1:T(2,128)S(1)}, bf16[8,64,128]{2,1,0:T(8,128)(2,1)S(1)}, s32[]{:T(128)}) %tuple.73), condition=%wide.while_cond, body=%wide.while_body.sunk | while | flops 2 | bytes 32873 | solution.py:77
  424.2 9.7 %while.28 = (s32[]{:T(128)}, bf16[64,4096]{1,0:T(8,128)(2,1)S(1)}, s32[8,2]{0,1:T(2,128)S(1)}, bf16[8,64,128]{2,1,0:T(8,128)(2,1)S(1)}, s32[]{:T(128)}) while((s32[]{:T(128)}, bf16[64,4096]{1,0:T(8,128)(2,1)S(1)}, s32[8,2]{0,1:T(2,128)S(1)}, bf16[8,64,128]{2,1,0:T(8,128)(2,1)S(1)}, s32[]{:T(128)}) %tuple.73), condition=%wide.while_cond, body=%wide.while_body.sunk | while | flops 2 | bytes 32873 | solution.py:77
  444.4 9.7 %while.28 = (s32[]{:T(128)}, bf16[64,4096]{1,0:T(8,128)(2,1)S(1)}, s32[8,2]{0,1:T(2,128)S(1)}, bf16[8,64,128]{2,1,0:T(8,128)(2,1)S(1)}, s32[]{:T(128)}) while((s32[]{:T(128)}, bf16[64,4096]{1,0:T(8,128)(2,1)S(1)}, s32[8,2]{0,1:T(2,128)S(1)}, bf16[8,64,128]{2,1,0:T(8,128)(2,1)S(1)}, s32[]{:T(128)}) %tuple.73), condition=%wide.while_cond, body=%wide.while_body.sunk | while | flops 2 | bytes 32873 | solution.py:77
  464.7 9.7 %while.28 = (s32[]{:T(128)}, bf16[64,4096]{1,0:T(8,128)(2,1)S(1)}, s32[8,2]{0,1:T(2,128)S(1)}, bf16[8,64,128]{2,1,0:T(8,128)(2,1)S(1)}, s32[]{:T(128)}) while((s32[]{:T(128)}, bf16[64,4096]{1,0:T(8,128)(2,1)S(1)}, s32[8,2]{0,1:T(2,128)S(1)}, bf16[8,64,128]{2,1,0:T(8,128)(2,1)S(1)}, s32[]{:T(128)}) %tuple.73), condition=%wide.while_cond, body=%wide.while_body.sunk | while | flops 2 | bytes 32873 | solution.py:77
  484.9 9.7 %while.28 = (s32[]{:T(128)}, bf16[64,4096]{1,0:T(8,128)(2,1)S(1)}, s32[8,2]{0,1:T(2,128)S(1)}, bf16[8,64,128]{2,1,0:T(8,128)(2,1)S(1)}, s32[]{:T(128)}) while((s32[]{:T(128)}, bf16[64,4096]{1,0:T(8,128)(2,1)S(1)}, s32[8,2]{0,1:T(2,128)S(1)}, bf16[8,64,128]{2,1,0:T(8,128)(2,1)S(1)}, s32[]{:T(128)}) %tuple.73), condition=%wide.while_cond, body=%wide.while_body.sunk | while | flops 2 | bytes 32873 | solution.py:77
  505.1 9.7 %while.28 = (s32[]{:T(128)}, bf16[64,4096]{1,0:T(8,128)(2,1)S(1)}, s32[8,2]{0,1:T(2,128)S(1)}, bf16[8,64,128]{2,1,0:T(8,128)(2,1)S(1)}, s32[]{:T(128)}) while((s32[]{:T(128)}, bf16[64,4096]{1,0:T(8,128)(2,1)S(1)}, s32[8,2]{0,1:T(2,128)S(1)}, bf16[8,64,128]{2,1,0:T(8,128)(2,1)S(1)}, s32[]{:T(128)}) %tuple.73), condition=%wide.while_cond, body=%wide.while_body.sunk | while | flops 2 | bytes 32873 | solution.py:77
  525.4 9.7 %while.28 = (s32[]{:T(128)}, bf16[64,4096]{1,0:T(8,128)(2,1)S(1)}, s32[8,2]{0,1:T(2,128)S(1)}, bf16[8,64,128]{2,1,0:T(8,128)(2,1)S(1)}, s32[]{:T(128)}) while((s32[]{:T(128)}, bf16[64,4096]{1,0:T(8,128)(2,1)S(1)}, s32[8,2]{0,1:T(2,128)S(1)}, bf16[8,64,128]{2,1,0:T(8,128)(2,1)S(1)}, s32[]{:T(128)}) %tuple.73), condition=%wide.while_cond, body=%wide.while_body.sunk | while | flops 2 | bytes 32873 | solution.py:77
  667.0 9.7 %while.28 = (s32[]{:T(128)}, bf16[64,4096]{1,0:T(8,128)(2,1)S(1)}, s32[8,2]{0,1:T(2,128)S(1)}, bf16[8,64,128]{2,1,0:T(8,128)(2,1)S(1)}, s32[]{:T(128)}) while((s32[]{:T(128)}, bf16[64,4096]{1,0:T(8,128)(2,1)S(1)}, s32[8,2]{0,1:T(2,128)S(1)}, bf16[8,64,128]{2,1,0:T(8,128)(2,1)S(1)}, s32[]{:T(128)}) %tuple.73), condition=%wide.while_cond, body=%wide.while_body.sunk | while | flops 2 | bytes 32873 | solution.py:77
  707.5 9.7 %while.28 = (s32[]{:T(128)}, bf16[64,4096]{1,0:T(8,128)(2,1)S(1)}, s32[8,2]{0,1:T(2,128)S(1)}, bf16[8,64,128]{2,1,0:T(8,128)(2,1)S(1)}, s32[]{:T(128)}) while((s32[]{:T(128)}, bf16[64,4096]{1,0:T(8,128)(2,1)S(1)}, s32[8,2]{0,1:T(2,128)S(1)}, bf16[8,64,128]{2,1,0:T(8,128)(2,1)S(1)}, s32[]{:T(128)}) %tuple.73), condition=%wide.while_cond, body=%wide.while_body.sunk | while | flops 2 | bytes 32873 | solution.py:77
  748.0 9.7 %while.28 = (s32[]{:T(128)}, bf16[64,4096]{1,0:T(8,128)(2,1)S(1)}, s32[8,2]{0,1:T(2,128)S(1)}, bf16[8,64,128]{2,1,0:T(8,128)(2,1)S(1)}, s32[]{:T(128)}) while((s32[]{:T(128)}, bf16[64,4096]{1,0:T(8,128)(2,1)S(1)}, s32[8,2]{0,1:T(2,128)S(1)}, bf16[8,64,128]{2,1,0:T(8,128)(2,1)S(1)}, s32[]{:T(128)}) %tuple.73), condition=%wide.while_cond, body=%wide.while_body.sunk | while | flops 2 | bytes 32873 | solution.py:77
  (1213 shorter events, 741.8 us)
Async XLA Ops:
  6.5 34.2 %all-gather.7.cloned.1.call-start = ((), (), s32[]{:S(2)}) async-start(), calls=%async_computation.1 | async-start | bytes 1310720 | tf_op jit(solution)/shard_map/all_gather | solution.py:24
  16.7 196.0 %all-gather.5.cloned.1.call-start = ((), (), s32[]{:S(2)}) async-start(), calls=%async_computation | async-start | bytes 17825792 | tf_op jit(solution)/shard_map/all_gather | solution.py:123
  43.0 169.7 %copy-start = (s32[32,2]{0,1:T(2,128)S(1)}, s32[32,2]{0,1:T(2,128)}, u32[]{:S(2)}) copy-start(s32[32,2]{0,1:T(2,128)} %param.7) | copy-start | bytes 772
  43.1 169.6 %copy-start.1 = (s32[32]{0:T(128)S(1)}, s32[32]{0:T(128)}, u32[]{:S(2)}) copy-start(s32[32]{0:T(128)} %param.6) | copy-start | bytes 388
Sparse Core Ops, SparseCore 0:
  16.8 23.9 all-gather.6
  119.4 93.2 all-gather.4
where the time goes:
time: 881 us; the launch traced here: 875 us
  local copies, waits for them, and re-layouts  390 us (44%)
  other arithmetic  182 us (21%)
  matrix products  120 us (14%)
  waiting for transfers between devices  117 us (13%)
  loops' own time  42.2 us (5%)
  between operations  13.5 us (2%)
  blocking collectives  10.1 us (1%)
    gather x768, local copies, waits for them, and re-layouts  307 us
    all_gather x1, waiting for transfers between devices, shards(): lax.all_gather(filtered, 'ang', axis=0, tiled=True)  93.4 us
    dot_general x1, matrix products, shards(): jnp.dot(whole_bins.reshape(-1, BINS).astype(jnp.float32), ramp_rows, prec...  76.2 us
    sub x32, other arithmetic, one_angle(): low_bin = (position // 16 - band_start[:, None])[:, None, :]  60.5 us
    sub x32, other arithmetic, one_angle(): 1.0 - upper_weight  60.4 us
    min x32, other arithmetic, one_angle(): band_start = jnp.minimum(corner // 16, BINS - BAND)  57.9 us
    dot_general x32, matrix products, one_angle(): jnp.einsum('tsb,tbp->tsp', band_rows, weights, preferred_element_type=jnp...  43.4 us
    another operation x1, loops' own time, one_block(): lax.scan(one_angle, start_sum, (filtered, geo_offsets, geo_steps))[0]  38.2 us
  transfers between devices with their start and end apart: 2, of which 2 were waited for; matrix products, arithmetic and copies ran while one was open for 0% of the time, Pallas kernels for 0%

commit v1 on v0

--- a/solution.py
+++ b/solution.py
@@ -120,7 +120,9 @@
     total_angles = angles_dev * ang_count
     row_first = lax.axis_index("ang") * rows_dev
     partial_value = project_block(
-        lax.all_gather(filtered, "ang", axis=0, tiled=True),
+        jnp.concatenate(
+            lax.all_to_all(jnp.stack([filtered] * lax.axis_size("ang")), "ang", 0, 0), axis=0
+        ),
         offsets,
         steps,
         row_first,

time: 881 us -> 1090 us (1.24)
  waiting for transfers between devices: 117 us -> 249 us
  local copies, waits for them, and re-layouts: 390 us -> 453 us
    all_to_all x0 -> x1, waiting for transfers between devices: none -> 224 us  [shards(): lax.all_to_all(jnp.stack([filtered] * lax.axis_size('ang')), 'ang', 0, 0)]
    all_gather x1 -> x0, waiting for transfers between devices: 93.4 us -> none  [shards(): lax.all_gather(filtered, 'ang', axis=0, tiled=True)]
    gather x768, local copies, waits for them, and re-layouts: 307 us -> 365 us
where the time goes in v1:
time: 1090 us; the launch traced here: 1080 us
  local copies, waits for them, and re-layouts  453 us (42%)
  waiting for transfers between devices  249 us (23%)
  other arithmetic  184 us (17%)
  matrix products  119 us (11%)
  loops' own time  45 us (4%)
  between operations  13.5 us (1%)
    gather x768, local copies, waits for them, and re-layouts  365 us
    all_to_all x1, waiting for transfers between devices, shards(): lax.all_to_all(jnp.stack([filtered] * lax.axis_size('ang')), 'ang', 0, 0)  224 us
    dot_general x1, matrix products, shards(): jnp.dot(whole_bins.reshape(-1, BINS).astype(jnp.float32), ramp_rows, prec...  75.5 us
    sub x32, other arithmetic, one_angle(): low_bin = (position // 16 - band_start[:, None])[:, None, :]  61.2 us
    sub x32, other arithmetic, one_angle(): 1.0 - upper_weight  61 us
    min x32, other arithmetic, one_angle(): band_start = jnp.minimum(corner // 16, BINS - BAND)  58.5 us
    dot_general x32, matrix products, one_angle(): jnp.einsum('tsb,tbp->tsp', band_rows, weights, preferred_element_type=jnp...  43.7 us
    another operation x1, loops' own time, one_block(): lax.scan(one_angle, start_sum, (filtered, geo_offsets, geo_steps))[0]  41 us
  transfers between devices with their start and end apart: 2, of which 2 were waited for; matrix products, arithmetic and copies ran while one was open for 0% of the time, Pallas kernels for 0%

profile of v1, /device:TPU:1, one launch (start us, length us, event | category | flops | bytes accessed | tf_op | source)
XLA Modules:
  0.0 1080.9 jit_solution(12556724441993494312)
XLA Ops:
  16.7 24.1 %all-gather.4.cloned.1.call-done = bf16[8,2,64,512]{3,2,1,0:T(8,128)(2,1)} async-done(((bf16[2,2,64,512]{3,2,1,0:T(8,128)(2,1)}), bf16[8,2,64,512]{3,2,1,0:T(8,128)(2,1)}) %all-gather.4.cloned.1.call-update) | async-done | bytes 1048592 | tf_op jit(solution)/shard_map/all_gather | solution.py:24
  43.0 75.5 %fusion.51 = bf16[4096,128]{0,1:T(8,128)(2,1)S(1)} fusion(bf16[128,4096]{1,0:T(8,128)(2,1)S(1)} %bitcast.60), kind=kOutput, calls=%fused_computation.89 | convolution fusion | flops 26122649600 | bytes 2097152 | tf_op jit(solution)/shard_map/dot_general | solution.py:108
  131.5 224.5 %all-to-all-done = bf16[16,2,64,4096]{3,2,1,0:T(8,128)(2,1)} async-done(((bf16[16,2,64,4096]{3,2,1,0:T(8,128)(2,1)}), bf16[16,2,64,4096]{3,2,1,0:T(8,128)(2,1)}, u32[]{:S(2)}, u32[]{:S(2)}) %all-to-all-start) | async-done | bytes 16777248 | tf_op jit(solution)/shard_map/all_to_all | solution.py:124
  356.0 710.4 %while.27 = (s32[]{:T(128)}, f32[8,64,1024]{2,1,0:T(8,128)S(1)}, bf16[32,64,4096]{2,1,0:T(8,128)(2,1)}, s32[32]{0:T(128)S(1)}, s32[32,2]{0,1:T(2,128)S(1)}, /*in...) while((s32[]{:T(128)}, f32[8,64,1024]{2,1,0:T(8,128)S(1)}, ...), condition=%wide.region_1.2_spmd.clone.clone, body=%wide.region_0.1_spmd.clone.clone.sunk | while | flops 141922896 | bytes 5694316 | solution.py:96
  363.4 11.5 %while.28 = (s32[]{:T(128)}, bf16[64,4096]{1,0:T(8,128)(2,1)S(1)}, s32[8,2]{0,1:T(2,128)S(1)}, bf16[8,64,128]{2,1,0:T(8,128)(2,1)S(1)}, s32[]{:T(128)}) while((s32[]{:T(128)}, bf16[64,4096]{1,0:T(8,128)(2,1)S(1)}, s32[8,2]{0,1:T(2,128)S(1)}, bf16[8,64,128]{2,1,0:T(8,128)(2,1)S(1)}, s32[]{:T(128)}) %tuple.73), condition=%wide.while_cond, body=%wide.while_body.sunk | while | flops 2 | bytes 32865 | solution.py:77
  385.6 11.5 %while.28 = (s32[]{:T(128)}, bf16[64,4096]{1,0:T(8,128)(2,1)S(1)}, s32[8,2]{0,1:T(2,128)S(1)}, bf16[8,64,128]{2,1,0:T(8,128)(2,1)S(1)}, s32[]{:T(128)}) while((s32[]{:T(128)}, bf16[64,4096]{1,0:T(8,128)(2,1)S(1)}, s32[8,2]{0,1:T(2,128)S(1)}, bf16[8,64,128]{2,1,0:T(8,128)(2,1)S(1)}, s32[]{:T(128)}) %tuple.73), condition=%wide.while_cond, body=%wide.while_body.sunk | while | flops 2 | bytes 32865 | solution.py:77
  407.8 11.5 %while.28 = (s32[]{:T(128)}, bf16[64,4096]{1,0:T(8,128)(2,1)S(1)}, s32[8,2]{0,1:T(2,128)S(1)}, bf16[8,64,128]{2,1,0:T(8,128)(2,1)S(1)}, s32[]{:T(128)}) while((s32[]{:T(128)}, bf16[64,4096]{1,0:T(8,128)(2,1)S(1)}, s32[8,2]{0,1:T(2,128)S(1)}, bf16[8,64,128]{2,1,0:T(8,128)(2,1)S(1)}, s32[]{:T(128)}) %tuple.73), condition=%wide.while_cond, body=%wide.while_body.sunk | while | flops 2 | bytes 32865 | solution.py:77
  430.0 11.5 %while.28 = (s32[]{:T(128)}, bf16[64,4096]{1,0:T(8,128)(2,1)S(1)}, s32[8,2]{0,1:T(2,128)S(1)}, bf16[8,64,128]{2,1,0:T(8,128)(2,1)S(1)}, s32[]{:T(128)}) while((s32[]{:T(128)}, bf16[64,4096]{1,0:T(8,128)(2,1)S(1)}, s32[8,2]{0,1:T(2,128)S(1)}, bf16[8,64,128]{2,1,0:T(8,128)(2,1)S(1)}, s32[]{:T(128)}) %tuple.73), condition=%wide.while_cond, body=%wide.while_body.sunk | while | flops 2 | bytes 32865 | solution.py:77
  452.2 11.5 %while.28 = (s32[]{:T(128)}, bf16[64,4096]{1,0:T(8,128)(2,1)S(1)}, s32[8,2]{0,1:T(2,128)S(1)}, bf16[8,64,128]{2,1,0:T(8,128)(2,1)S(1)}, s32[]{:T(128)}) while((s32[]{:T(128)}, bf16[64,4096]{1,0:T(8,128)(2,1)S(1)}, s32[8,2]{0,1:T(2,128)S(1)}, bf16[8,64,128]{2,1,0:T(8,128)(2,1)S(1)}, s32[]{:T(128)}) %tuple.73), condition=%wide.while_cond, body=%wide.while_body.sunk | while | flops 2 | bytes 32865 | solution.py:77
  474.4 11.5 %while.28 = (s32[]{:T(128)}, bf16[64,4096]{1,0:T(8,128)(2,1)S(1)}, s32[8,2]{0,1:T(2,128)S(1)}, bf16[8,64,128]{2,1,0:T(8,128)(2,1)S(1)}, s32[]{:T(128)}) while((s32[]{:T(128)}, bf16[64,4096]{1,0:T(8,128)(2,1)S(1)}, s32[8,2]{0,1:T(2,128)S(1)}, bf16[8,64,128]{2,1,0:T(8,128)(2,1)S(1)}, s32[]{:T(128)}) %tuple.73), condition=%wide.while_cond, body=%wide.while_body.sunk | while | flops 2 | bytes 32865 | solution.py:77
  496.6 11.5 %while.28 = (s32[]{:T(128)}, bf16[64,4096]{1,0:T(8,128)(2,1)S(1)}, s32[8,2]{0,1:T(2,128)S(1)}, bf16[8,64,128]{2,1,0:T(8,128)(2,1)S(1)}, s32[]{:T(128)}) while((s32[]{:T(128)}, bf16[64,4096]{1,0:T(8,128)(2,1)S(1)}, s32[8,2]{0,1:T(2,128)S(1)}, bf16[8,64,128]{2,1,0:T(8,128)(2,1)S(1)}, s32[]{:T(128)}) %tuple.73), condition=%wide.while_cond, body=%wide.while_body.sunk | while | flops 2 | bytes 32865 | solution.py:77
  518.8 11.5 %while.28 = (s32[]{:T(128)}, bf16[64,4096]{1,0:T(8,128)(2,1)S(1)}, s32[8,2]{0,1:T(2,128)S(1)}, bf16[8,64,128]{2,1,0:T(8,128)(2,1)S(1)}, s32[]{:T(128)}) while((s32[]{:T(128)}, bf16[64,4096]{1,0:T(8,128)(2,1)S(1)}, s32[8,2]{0,1:T(2,128)S(1)}, bf16[8,64,128]{2,1,0:T(8,128)(2,1)S(1)}, s32[]{:T(128)}) %tuple.73), condition=%wide.while_cond, body=%wide.while_body.sunk | while | flops 2 | bytes 32865 | solution.py:77
  541.0 11.5 %while.28 = (s32[]{:T(128)}, bf16[64,4096]{1,0:T(8,128)(2,1)S(1)}, s32[8,2]{0,1:T(2,128)S(1)}, bf16[8,64,128]{2,1,0:T(8,128)(2,1)S(1)}, s32[]{:T(128)}) while((s32[]{:T(128)}, bf16[64,4096]{1,0:T(8,128)(2,1)S(1)}, s32[8,2]{0,1:T(2,128)S(1)}, bf16[8,64,128]{2,1,0:T(8,128)(2,1)S(1)}, s32[]{:T(128)}) %tuple.73), condition=%wide.while_cond, body=%wide.while_body.sunk | while | flops 2 | bytes 32865 | solution.py:77
  563.2 11.5 %while.28 = (s32[]{:T(128)}, bf16[64,4096]{1,0:T(8,128)(2,1)S(1)}, s32[8,2]{0,1:T(2,128)S(1)}, bf16[8,64,128]{2,1,0:T(8,128)(2,1)S(1)}, s32[]{:T(128)}) while((s32[]{:T(128)}, bf16[64,4096]{1,0:T(8,128)(2,1)S(1)}, s32[8,2]{0,1:T(2,128)S(1)}, bf16[8,64,128]{2,1,0:T(8,128)(2,1)S(1)}, s32[]{:T(128)}) %tuple.73), condition=%wide.while_cond, body=%wide.while_body.sunk | while | flops 2 | bytes 32865 | solution.py:77
  585.4 11.5 %while.28 = (s32[]{:T(128)}, bf16[64,4096]{1,0:T(8,128)(2,1)S(1)}, s32[8,2]{0,1:T(2,128)S(1)}, bf16[8,64,128]{2,1,0:T(8,128)(2,1)S(1)}, s32[]{:T(128)}) while((s32[]{:T(128)}, bf16[64,4096]{1,0:T(8,128)(2,1)S(1)}, s32[8,2]{0,1:T(2,128)S(1)}, bf16[8,64,128]{2,1,0:T(8,128)(2,1)S(1)}, s32[]{:T(128)}) %tuple.73), condition=%wide.while_cond, body=%wide.while_body.sunk | while | flops 2 | bytes 32865 | solution.py:77
  607.6 11.5 %while.28 = (s32[]{:T(128)}, bf16[64,4096]{1,0:T(8,128)(2,1)S(1)}, s32[8,2]{0,1:T(2,128)S(1)}, bf16[8,64,128]{2,1,0:T(8,128)(2,1)S(1)}, s32[]{:T(128)}) while((s32[]{:T(128)}, bf16[64,4096]{1,0:T(8,128)(2,1)S(1)}, s32[8,2]{0,1:T(2,128)S(1)}, bf16[8,64,128]{2,1,0:T(8,128)(2,1)S(1)}, s32[]{:T(128)}) %tuple.73), condition=%wide.while_cond, body=%wide.while_body.sunk | while | flops 2 | bytes 32865 | solution.py:77
  629.8 11.5 %while.28 = (s32[]{:T(128)}, bf16[64,4096]{1,0:T(8,128)(2,1)S(1)}, s32[8,2]{0,1:T(2,128)S(1)}, bf16[8,64,128]{2,1,0:T(8,128)(2,1)S(1)}, s32[]{:T(128)}) while((s32[]{:T(128)}, bf16[64,4096]{1,0:T(8,128)(2,1)S(1)}, s32[8,2]{0,1:T(2,128)S(1)}, bf16[8,64,128]{2,1,0:T(8,128)(2,1)S(1)}, s32[]{:T(128)}) %tuple.73), condition=%wide.while_cond, body=%wide.while_body.sunk | while | flops 2 | bytes 32865 | solution.py:77
  652.0 11.5 %while.28 = (s32[]{:T(128)}, bf16[64,4096]{1,0:T(8,128)(2,1)S(1)}, s32[8,2]{0,1:T(2,128)S(1)}, bf16[8,64,128]{2,1,0:T(8,128)(2,1)S(1)}, s32[]{:T(128)}) while((s32[]{:T(128)}, bf16[64,4096]{1,0:T(8,128)(2,1)S(1)}, s32[8,2]{0,1:T(2,128)S(1)}, bf16[8,64,128]{2,1,0:T(8,128)(2,1)S(1)}, s32[]{:T(128)}) %tuple.73), condition=%wide.while_cond, body=%wide.while_body.sunk | while | flops 2 | bytes 32865 | solution.py:77
  674.2 11.5 %while.28 = (s32[]{:T(128)}, bf16[64,4096]{1,0:T(8,128)(2,1)S(1)}, s32[8,2]{0,1:T(2,128)S(1)}, bf16[8,64,128]{2,1,0:T(8,128)(2,1)S(1)}, s32[]{:T(128)}) while((s32[]{:T(128)}, bf16[64,4096]{1,0:T(8,128)(2,1)S(1)}, s32[8,2]{0,1:T(2,128)S(1)}, bf16[8,64,128]{2,1,0:T(8,128)(2,1)S(1)}, s32[]{:T(128)}) %tuple.73), condition=%wide.while_cond, body=%wide.while_body.sunk | while | flops 2 | bytes 32865 | solution.py:77
  696.4 11.5 %while.28 = (s32[]{:T(128)}, bf16[64,4096]{1,0:T(8,128)(2,1)S(1)}, s32[8,2]{0,1:T(2,128)S(1)}, bf16[8,64,128]{2,1,0:T(8,128)(2,1)S(1)}, s32[]{:T(128)}) while((s32[]{:T(128)}, bf16[64,4096]{1,0:T(8,128)(2,1)S(1)}, s32[8,2]{0,1:T(2,128)S(1)}, bf16[8,64,128]{2,1,0:T(8,128)(2,1)S(1)}, s32[]{:T(128)}) %tuple.73), condition=%wide.while_cond, body=%wide.while_body.sunk | while | flops 2 | bytes 32865 | solution.py:77
  718.6 11.5 %while.28 = (s32[]{:T(128)}, bf16[64,4096]{1,0:T(8,128)(2,1)S(1)}, s32[8,2]{0,1:T(2,128)S(1)}, bf16[8,64,128]{2,1,0:T(8,128)(2,1)S(1)}, s32[]{:T(128)}) while((s32[]{:T(128)}, bf16[64,4096]{1,0:T(8,128)(2,1)S(1)}, s32[8,2]{0,1:T(2,128)S(1)}, bf16[8,64,128]{2,1,0:T(8,128)(2,1)S(1)}, s32[]{:T(128)}) %tuple.73), condition=%wide.while_cond, body=%wide.while_body.sunk | while | flops 2 | bytes 32865 | solution.py:77
  740.8 11.5 %while.28 = (s32[]{:T(128)}, bf16[64,4096]{1,0:T(8,128)(2,1)S(1)}, s32[8,2]{0,1:T(2,128)S(1)}, bf16[8,64,128]{2,1,0:T(8,128)(2,1)S(1)}, s32[]{:T(128)}) while((s32[]{:T(128)}, bf16[64,4096]{1,0:T(8,128)(2,1)S(1)}, s32[8,2]{0,1:T(2,128)S(1)}, bf16[8,64,128]{2,1,0:T(8,128)(2,1)S(1)}, s32[]{:T(128)}) %tuple.73), condition=%wide.while_cond, body=%wide.while_body.sunk | while | flops 2 | bytes 32865 | solution.py:77
  763.0 11.5 %while.28 = (s32[]{:T(128)}, bf16[64,4096]{1,0:T(8,128)(2,1)S(1)}, s32[8,2]{0,1:T(2,128)S(1)}, bf16[8,64,128]{2,1,0:T(8,128)(2,1)S(1)}, s32[]{:T(128)}) while((s32[]{:T(128)}, bf16[64,4096]{1,0:T(8,128)(2,1)S(1)}, s32[8,2]{0,1:T(2,128)S(1)}, bf16[8,64,128]{2,1,0:T(8,128)(2,1)S(1)}, s32[]{:T(128)}) %tuple.73), condition=%wide.while_cond, body=%wide.while_body.sunk | while | flops 2 | bytes 32865 | solution.py:77
  785.2 11.5 %while.28 = (s32[]{:T(128)}, bf16[64,4096]{1,0:T(8,128)(2,1)S(1)}, s32[8,2]{0,1:T(2,128)S(1)}, bf16[8,64,128]{2,1,0:T(8,128)(2,1)S(1)}, s32[]{:T(128)}) while((s32[]{:T(128)}, bf16[64,4096]{1,0:T(8,128)(2,1)S(1)}, s32[8,2]{0,1:T(2,128)S(1)}, bf16[8,64,128]{2,1,0:T(8,128)(2,1)S(1)}, s32[]{:T(128)}) %tuple.73), condition=%wide.while_cond, body=%wide.while_body.sunk | while | flops 2 | bytes 32865 | solution.py:77
  (1213 shorter events, 836.7 us)
Async XLA Ops:
  6.5 34.2 %all-gather.4.cloned.1.call-start = ((), (), s32[]{:S(2)}) async-start(), calls=%async_computation.1 | async-start | bytes 1310720 | tf_op jit(solution)/shard_map/all_gather | solution.py:24
  124.6 231.4 %copy-start = (s32[32,2]{0,1:T(2,128)S(1)}, s32[32,2]{0,1:T(2,128)}, u32[]{:S(2)}) copy-start(s32[32,2]{0,1:T(2,128)} %param.7) | copy-start | bytes 772
  124.6 231.4 %copy-start.1 = (s32[32]{0:T(128)S(1)}, s32[32]{0:T(128)}, u32[]{:S(2)}) copy-start(s32[32]{0:T(128)} %param.6) | copy-start | bytes 388
  124.6 231.4 %all-to-all-start = ((bf16[16,2,64,4096]{3,2,1,0:T(8,128)(2,1)}), bf16[16,2,64,4096]{3,2,1,0:T(8,128)(2,1)}, u32[]{:S(2)}, u32[]{:S(2)}) async-start(bf16[16,2,64,4096]{3,2,1,0:T(8,128)(2,1)} %stack.3), calls=%async_computation | async-start | bytes 33554432 | tf_op jit(solution)/shard_map/all_to_all | solution.py:124
Sparse Core Ops, SparseCore 0:
  16.8 23.8 all-gather.3
